TPU v7x, 32 devices: a whole 2x2x4 slice. The times are simulated.
32 devices in a mesh: img: 8 (over z, x), head: 4 (over y, core).
Axes of the slice: x: 2, y: 2, z: 4, core: 2. Of those that a mesh axis runs over, the one named last changes fastest.
Arguments:
- inputs: bfloat16 [2048, 1280], P('img'), may hold values from -6 to 6
- middle: bfloat16 [2048, 1280], P('img'), may hold values from -6 to 6
- out_grad: bfloat16 [2048, 1280], P('img'), may hold values from -6 to 6
- cached_maps: bfloat16 [8, 16, 256, 256], P('img', 'head'), may hold values from 0 to 1, as said below
- w_value: bfloat16 [1280, 1280], P(None, 'head'), may hold values from -0.15625 to 0.15625
- w_out: bfloat16 [1280, 1280], P('head'), may hold values from -0.15625 to 0.15625
- w_up: bfloat16 [1280, 2560], P(None, 'head'), may hold values from -0.15625 to 0.15625
- w_down: bfloat16 [2560, 1280], P('head'), may hold values from -0.125 to 0.125
Outputs:
- in_grad: bfloat16 [2048, 1280], P(('img', 'head'))
- grad_value: float32 [1280, 1280], P('img', 'head')
- grad_out: float32 [1280, 1280], P('head', 'img')
- grad_up: float32 [1280, 2560], P('img', 'head')
- grad_down: float32 [2560, 1280], P('head', 'img')
Inputs may be any that keep to these rules, and one draw needn't show every extreme that they name: `cached_maps`: every row of every map is positive and sums to one up to rounding.
All inputs are finite; a program needn't handle non-finite values.
Results may differ from a plain program's by a relative error of at most 0.0069.
Values may be sent and summed in bfloat16 or wider, within the bound.
A program may use at most 128 MiB of HBM per device.

v0:
```python
import jax
import jax.numpy as jnp
from jax import lax
from jax.experimental import pallas as pl
from jax.experimental.pallas import tpu as pltpu
from jax.sharding import PartitionSpec as P


def norm_rows(rows):
    centre = rows - jnp.mean(rows, axis=-1, keepdims=True)
    spread = jnp.mean(centre * centre, axis=-1, keepdims=True)
    return centre * lax.rsqrt(spread + 1e-06)


def norm_back(rows, grad):
    centre = rows - jnp.mean(rows, axis=-1, keepdims=True)
    factor = lax.rsqrt(jnp.mean(centre * centre, axis=-1, keepdims=True) + 1e-06)
    normed = centre * factor
    return factor * (
        grad
        - jnp.mean(grad, axis=-1, keepdims=True)
        - normed * jnp.mean(grad * normed, axis=-1, keepdims=True)
    )


def gelu_tanh(pre):
    return jax.nn.gelu(pre, approximate=True)


def on_device(inputs, middle, out_grad, cached_maps, w_value, w_out, w_up, w_down):
    tok_rows = inputs.shape[0]
    heads_here = cached_maps.shape[1]
    share = tok_rows // lax.axis_size("head")
    first = lax.axis_index("head") * share
    maps_here = cached_maps[0]
    normed_in = norm_rows(inputs.astype(jnp.float32)).astype(jnp.bfloat16)
    values = jnp.dot(normed_in, w_value, preferred_element_type=jnp.float32).astype(jnp.bfloat16)
    head_size = values.shape[1] // heads_here
    attended = jnp.einsum(
        "htk,khd->thd",
        maps_here,
        values.reshape(tok_rows, heads_here, head_size),
        preferred_element_type=jnp.float32,
    )
    attended = attended.astype(jnp.bfloat16).reshape(tok_rows, -1)
    middle_f = middle.astype(jnp.float32)
    normed_mid = norm_rows(middle_f).astype(jnp.bfloat16)
    pre = jnp.dot(normed_mid, w_up, preferred_element_type=jnp.float32)
    hidden = gelu_tanh(pre).astype(jnp.bfloat16)
    hidden_grad = jnp.einsum("td,fd->tf", out_grad, w_down, preferred_element_type=jnp.float32)
    pre_grad = jax.vjp(gelu_tanh, pre)[1](hidden_grad)[0].astype(jnp.bfloat16)
    down_term = jnp.einsum("tf,td->fd", hidden, out_grad, preferred_element_type=jnp.float32)
    mid_part = jnp.einsum("tf,df->td", pre_grad, w_up, preferred_element_type=jnp.float32)
    out_rows = lax.dynamic_slice_in_dim(out_grad, first, share, 0).astype(jnp.float32)
    mid_share = lax.psum_scatter(mid_part, "head", scatter_dimension=0, tiled=True)
    mid_own = out_rows + norm_back(lax.dynamic_slice_in_dim(middle_f, first, share, 0), mid_share)
    mid_grad_b = lax.all_gather(mid_own.astype(jnp.bfloat16), "head", axis=0, tiled=True)
    outproj_term = jnp.einsum("te,td->ed", attended, mid_grad_b, preferred_element_type=jnp.float32)
    att_grad = jnp.einsum(
        "td,ed->te", mid_grad_b, w_out, preferred_element_type=jnp.float32
    ).astype(jnp.bfloat16)
    value_grad = jnp.einsum(
        "htk,thd->khd",
        maps_here,
        att_grad.reshape(tok_rows, heads_here, head_size),
        preferred_element_type=jnp.float32,
    )
    value_grad = value_grad.astype(jnp.bfloat16).reshape(tok_rows, -1)
    input_part = jnp.einsum("te,de->td", value_grad, w_value, preferred_element_type=jnp.float32)
    inputs_own = lax.dynamic_slice_in_dim(inputs, first, share, 0).astype(jnp.float32)
    input_share = lax.psum_scatter(input_part, "head", scatter_dimension=0, tiled=True)
    in_grad = (mid_own + norm_back(inputs_own, input_share)).astype(jnp.bfloat16)
    picked = normed_mid
    up_term = jnp.einsum("tr,tf->rf", picked, pre_grad, preferred_element_type=jnp.float32)
    picked = normed_in
    value_term = jnp.einsum("tr,te->re", picked, value_grad, preferred_element_type=jnp.float32)
    grad_down, grad_out = (
        lax.psum_scatter(down_term, "img", scatter_dimension=1, tiled=True),
        lax.psum_scatter(outproj_term, "img", scatter_dimension=1, tiled=True),
    )
    grad_up, grad_value = (
        lax.psum_scatter(up_term, "img", scatter_dimension=0, tiled=True),
        lax.psum_scatter(value_term, "img", scatter_dimension=0, tiled=True),
    )
    return (in_grad, grad_value, grad_out, grad_up, grad_down)


MESH = pl.DeviceIdType.MESH
F32 = jnp.float32
BF16 = jnp.bfloat16
EARLY = 128
GELU_C = 0.7978845608028654


def dot_nn(a, b):
    return lax.dot_general(a, b, (((1,), (0,)), ((), ())), preferred_element_type=F32)


def dot_nt(a, b):
    return lax.dot_general(a, b, (((1,), (1,)), ((), ())), preferred_element_type=F32)


def dot_tn(a, b):
    return lax.dot_general(a, b, (((0,), (0,)), ((), ())), preferred_element_type=F32)


def gelu_and_slope(pre):
    square = pre * pre
    tanh = jnp.tanh(GELU_C * pre * (1.0 + 0.044715 * square))
    half = 0.5 * (1.0 + tanh)
    slope = half + 0.5 * pre * (1.0 - tanh * tanh) * (GELU_C * (1.0 + 3 * 0.044715 * square))
    return pre * half, slope


def block_kernel(
    inputs_h, middle_h, out_grad_h, maps_h, w_value_h, w_out_h, w_up_h, w_down_h,
    in_grad, mlp_sum, att_sum,
    inputs, middle, out_grad, maps, w_value_t, w_out, w_up, w_down,
    nmt, ogt, nint, midbt, hid, prg, attd, vgr, mp, rs1, rs2, midb, mid_own,
    a_buf, b_buf, att_buf, xr_a, xr_b, xr, zr_a, zs_a, zr_b, zs_b, zr2, zs2, xs_a,
    local_sem, send_sem, recv_sem,
):
    tok, width = inputs.shape
    share = tok // 4
    heads_here = maps.shape[0]
    local = attd.shape[1]
    hdim = local // heads_here
    ff = hid.shape[1]
    early = a_buf.shape[2] // 2
    late = ff - early
    piece = mlp_sum.shape[0]
    img = lax.axis_index("img")
    head = lax.axis_index("head")
    z = img // 2
    x = img % 2
    upper = z // 2
    depth = z % 2 * (1 - 2 * upper) + upper
    x_peer = {"img": z * 2 + (1 - x)}
    side_peer = {"img": (z + 1 - 2 * (z % 2)) * 2 + x}
    across_peer = {"img": (3 - z) * 2 + x}
    head_ids = [(head + p) % 4 for p in (1, 2, 3)]

    def copy(src, dst, sem, peer):
        return pltpu.make_async_remote_copy(
            src_ref=src, dst_ref=dst, send_sem=send_sem.at[sem], recv_sem=recv_sem.at[sem],
            device_id=peer, device_id_type=MESH,
        )

    barrier = pltpu.get_barrier_semaphore()
    for peer in [x_peer, side_peer, across_peer] + [{"head": h} for h in head_ids]:
        pl.semaphore_signal(barrier, inc=1, device_id=peer, device_id_type=MESH)
    loads = [
        pltpu.make_async_copy(src, dst, local_sem.at[i])
        for i, (src, dst) in enumerate([
            (middle_h, middle), (w_up_h, w_up), (out_grad_h, out_grad), (w_down_h, w_down),
            (inputs_h, inputs), (w_value_h, w_value_t), (maps_h, maps), (w_out_h, w_out),
        ])
    ]
    for c in loads:
        c.start()
    loads[0].wait()
    normed = norm_rows(middle[...].astype(F32)).astype(BF16)
    nmt[...] = normed.T
    loads[2].wait()
    ogt[...] = out_grad[...].T
    loads[1].wait()
    pre = dot_nn(normed, w_up[...])
    value, slope = gelu_and_slope(pre)
    hid[...] = value.astype(BF16)
    loads[3].wait()
    prg[...] = (slope * dot_nt(out_grad[...], w_down[...])).astype(BF16)

    def scatter(slot, landing, first_sem):
        return [
            copy(mp.at[slot, pl.ds(pl.multiple_of(h * share, share), share)], landing.at[p], first_sem + p, {"head": h})
            for p, h in enumerate(head_ids)
        ]

    own = pl.ds(pl.multiple_of(head * share, share), share)

    def actual(c):
        return c * (1 - 2 * upper) + 3 * upper

    def chunk(c, at_x):
        return pl.ds(pl.multiple_of((actual(c) * 2 + at_x) * piece, piece), piece)

    def exchange(buf, zr, zs, first_sem):
        ends = [copy(buf.at[c], zr.at[i], first_sem + i, side_peer) for i, c in enumerate((3, 2, 1))]
        cross = [copy(zs.at[i], zr.at[3 + i], first_sem + 3 + i, across_peer) for i in range(2)]
        back = copy(zs.at[2], zr.at[5], first_sem + 5, side_peer)
        return ends, cross, back

    ends_a, cross_a, back_a = exchange(a_buf, zr_a, zs_a, 18)
    ends_b, cross_b, back_b = exchange(b_buf, zr_b, zs_b, 24)
    ends2, cross2, back2 = exchange(att_buf, zr2, zs2, 30)

    def at_end(start):
        @pl.when(depth == 0)
        def _():
            start()

    def add(buf, zs, zr, slot, c, i):
        zs[slot] = (buf[c].astype(F32) + zr[i].astype(F32)).astype(BF16)

    pl.semaphore_wait(barrier, 6)
    order = (3, 2, 1 - depth, depth)
    x_b = []
    for i, c in enumerate(order):
        rows = chunk(c, 1 - x)
        b_buf[4 + c, :, 0:late] = dot_nn(ogt[rows], hid[:, early:ff]).astype(BF16)
        b_buf[4 + c, :, late:2 * late] = dot_nn(nmt[rows], prg[:, early:ff]).astype(BF16)
        x_b.append(copy(b_buf.at[4 + c], xr_b.at[i], 9 + i, x_peer))
        x_b[i].start()
        c = 3 - i
        rows = pl.ds(pl.multiple_of(actual(c) * 2 * piece, piece), 2 * piece)
        a_buf[c, :, 0:early] = dot_nn(ogt[rows], hid[:, 0:early]).astype(BF16)
        a_buf[c, :, early:2 * early] = dot_nn(nmt[rows], prg[:, 0:early]).astype(BF16)
        if i < 3:
            at_end(ends_a[i].start)
        if i == 0:
            mp[0] = dot_nt(prg[...], w_up[...]).astype(BF16)
            scatter1 = scatter(0, rs1, 0)
            for k in scatter1:
                k.start()
    for c in (3, 2, 1, 0):
        rows = chunk(c, x)
        b_buf[c, :, 0:late] = dot_nn(ogt[rows], hid[:, early:ff]).astype(BF16)
        b_buf[c, :, late:2 * late] = dot_nn(nmt[rows], prg[:, early:ff]).astype(BF16)

    for c in loads[4:]:
        c.wait()
    normed_in = norm_rows(inputs[...].astype(F32)).astype(BF16)
    nint[...] = normed_in.T
    values = dot_nt(normed_in, w_value_t[...]).astype(BF16)
    column = lax.broadcasted_iota(jnp.int32, (tok, local), 1)

    def own_columns(array, h):
        keep = (column >= h * hdim) & (column < (h + 1) * hdim)
        return jnp.where(keep, array, jnp.zeros_like(array))

    total = dot_nn(maps[0], own_columns(values, 0))
    for h in range(1, heads_here):
        total = total + dot_nn(maps[h], own_columns(values, h))
    attd[...] = total.astype(BF16)

    def pass_on(buf, zr, zs, ends, cross, i):
        ends[i].wait_recv()
        add(buf, zs, zr, i, 3 - i, i)
        cross[i].start()

    def give_back(buf, zr, zs, cross, back):
        cross[0].wait_recv()
        add(buf, zs, zr, 2, 0, 3)
        back.start()

    @pl.when(depth == 1)
    def _():
        pass_on(a_buf, zr_a, zs_a, ends_a, cross_a, 0)

    for c in scatter1:
        c.wait_recv()
    grad_sum = mp[0, own].astype(F32) + rs1[0].astype(F32) + rs1[1].astype(F32) + rs1[2].astype(F32)
    mid_rows = out_grad[own].astype(F32) + norm_back(middle[own].astype(F32), grad_sum)
    mid_own[...] = mid_rows
    midb[own] = mid_rows.astype(BF16)
    spread = [copy(midb.at[own], midb.at[own], 3 + p, {"head": h}) for p, h in enumerate(head_ids)]
    for c in spread:
        c.start()

    def settle_b(i):
        c = order[i]
        x_b[i].wait_recv()
        b_buf[c] = (b_buf[c].astype(F32) + xr_b[i].astype(F32)).astype(BF16)
        if i < 3:
            at_end(ends_b[i].start)

    settle_b(0)

    @pl.when(depth == 1)
    def _():
        pass_on(a_buf, zr_a, zs_a, ends_a, cross_a, 1)
        give_back(a_buf, zr_a, zs_a, cross_a, back_a)

    x_a = copy(xs_a.at[1 - x], xr_a, 13, x_peer)

    def split_a(total):
        xs_a[0] = total[0:piece].astype(BF16)
        xs_a[1] = total[piece:2 * piece].astype(BF16)

    @pl.when(depth == 1)
    def _():
        ends_a[2].wait_recv()
        cross_a[1].wait_recv()
        split_a(a_buf[1].astype(F32) + zr_a[2].astype(F32) + zr_a[4].astype(F32))
        x_a.start()

    @pl.when(depth == 0)
    def _():
        back_a.wait_recv()
        split_a(a_buf[0].astype(F32) + zr_a[5].astype(F32))
        x_a.start()

    settle_b(1)

    @pl.when(depth == 1)
    def _():
        pass_on(b_buf, zr_b, zs_b, ends_b, cross_b, 0)

    for c in spread:
        c.wait_recv()
    att_grad = dot_nt(midb[...], w_out[...]).astype(BF16)
    total = dot_tn(maps[0], own_columns(att_grad, 0))
    for h in range(1, heads_here):
        total = total + dot_tn(maps[h], own_columns(att_grad, h))
    vgr[...] = total.astype(BF16)
    midbt[...] = midb[...].T

    x_att = []
    for i, c in enumerate(order):
        rows = chunk(c, 1 - x)
        att_buf[4 + c, :, 0:local] = dot_nn(midbt[rows], attd[...]).astype(BF16)
        att_buf[4 + c, :, local:2 * local] = dot_nn(nint[rows], vgr[...]).astype(BF16)
        x_att.append(copy(att_buf.at[4 + c], xr.at[i], 14 + i, x_peer))
        x_att[i].start()
    mp[1] = dot_nn(vgr[...], w_value_t[...]).astype(BF16)
    scatter2 = scatter(1, rs2, 6)
    for c in scatter2:
        c.start()
    settle_b(2)

    @pl.when(depth == 1)
    def _():
        pass_on(b_buf, zr_b, zs_b, ends_b, cross_b, 1)
        give_back(b_buf, zr_b, zs_b, cross_b, back_b)

    for c in (3, 2, 1, 0):
        rows = chunk(c, x)
        att_buf[c, :, 0:local] = dot_nn(midbt[rows], attd[...]).astype(BF16)
        att_buf[c, :, local:2 * local] = dot_nn(nint[rows], vgr[...]).astype(BF16)

    settle_b(3)

    def settle_att(i):
        c = order[i]
        x_att[i].wait_recv()
        att_buf[c] = (att_buf[c].astype(F32) + xr[i].astype(F32)).astype(BF16)
        if i < 3:
            at_end(ends2[i].start)

    settle_att(0)
    for c in scatter2:
        c.wait_recv()
    grad_sum = mp[1, own].astype(F32) + rs2[0].astype(F32) + rs2[1].astype(F32) + rs2[2].astype(F32)
    in_grad[...] = (mid_own[...] + norm_back(inputs[own].astype(F32), grad_sum)).astype(BF16)
    x_a.wait_recv()
    total = xs_a[x].astype(F32) + xr_a[...].astype(F32)
    mlp_sum[:, 0:early] = total[:, 0:early]
    mlp_sum[:, ff:ff + early] = total[:, early:2 * early]
    settle_att(1)

    @pl.when(depth == 1)
    def _():
        pass_on(att_buf, zr2, zs2, ends2, cross2, 0)

    settle_att(2)

    @pl.when(depth == 1)
    def _():
        pass_on(att_buf, zr2, zs2, ends2, cross2, 1)
        give_back(att_buf, zr2, zs2, cross2, back2)

    settle_att(3)

    def put_b(total):
        mlp_sum[:, early:ff] = total[:, 0:late]
        mlp_sum[:, ff + early:2 * ff] = total[:, late:2 * late]

    @pl.when(depth == 1)
    def _():
        ends_b[2].wait_recv()
        cross_b[1].wait_recv()
        put_b(b_buf[1].astype(F32) + zr_b[2].astype(F32) + zr_b[4].astype(F32))
        ends2[2].wait_recv()
        cross2[1].wait_recv()
        att_sum[...] = att_buf[1].astype(F32) + zr2[2].astype(F32) + zr2[4].astype(F32)
        for c in cross_a + [back_a] + cross_b + [back_b] + cross2 + [back2]:
            c.wait_send()

    @pl.when(depth == 0)
    def _():
        back_b.wait_recv()
        put_b(b_buf[0].astype(F32) + zr_b[5].astype(F32))
        back2.wait_recv()
        att_sum[...] = att_buf[0].astype(F32) + zr2[5].astype(F32)
        for c in ends_a + ends_b + ends2:
            c.wait_send()

    for c in scatter1 + spread + scatter2 + x_b + [x_a] + x_att:
        c.wait_send()


def split_kernel(in_grad, mlp_sum, att_sum, in_grad_out, value_rows, out_rows_t, up_rows, down_rows_t):
    local, ff = value_rows.shape[1], up_rows.shape[1]
    in_grad_out[...] = in_grad[...]
    down_rows_t[...] = mlp_sum[:, 0:ff]
    up_rows[...] = mlp_sum[:, ff:2 * ff]
    out_rows_t[...] = att_sum[:, 0:local]
    value_rows[...] = att_sum[:, local:2 * local]


def on_device_fused(inputs, middle, out_grad, cached_maps, w_value, w_out, w_up, w_down):
    tok, width = inputs.shape
    local, ff = w_value.shape[1], w_up.shape[1]
    heads_here = cached_maps.shape[1]
    piece = width // lax.axis_size("img")
    share = tok // 4
    late = ff - EARLY
    vmem = pl.BlockSpec(memory_space=pltpu.VMEM)
    shape = jax.ShapeDtypeStruct
    sums = pl.pallas_call(
        block_kernel,
        out_shape=(
            shape((share, width), BF16),
            shape((piece, 2 * ff), F32),
            shape((piece, 2 * local), F32),
        ),
        in_specs=[pl.BlockSpec(memory_space=pl.ANY)] * 8,
        out_specs=(vmem,) * 3,
        scratch_shapes=[
            pltpu.VMEM((tok, width), BF16),
            pltpu.VMEM((tok, width), BF16),
            pltpu.VMEM((tok, width), BF16),
            pltpu.VMEM((heads_here, tok, tok), BF16),
            pltpu.VMEM((local, width), BF16),
            pltpu.VMEM((local, width), BF16),
            pltpu.VMEM((width, ff), BF16),
            pltpu.VMEM((ff, width), BF16),
            pltpu.VMEM((width, tok), BF16),
            pltpu.VMEM((width, tok), BF16),
            pltpu.VMEM((width, tok), BF16),
            pltpu.VMEM((width, tok), BF16),
            pltpu.VMEM((tok, ff), BF16),
            pltpu.VMEM((tok, ff), BF16),
            pltpu.VMEM((tok, local), BF16),
            pltpu.VMEM((tok, local), BF16),
            pltpu.VMEM((2, tok, width), BF16),
            pltpu.VMEM((3, share, width), BF16),
            pltpu.VMEM((3, share, width), BF16),
            pltpu.VMEM((tok, width), BF16),
            pltpu.VMEM((share, width), F32),
            pltpu.VMEM((4, 2 * piece, 2 * EARLY), BF16),
            pltpu.VMEM((8, piece, 2 * late), BF16),
            pltpu.VMEM((8, piece, 2 * local), BF16),
            pltpu.VMEM((piece, 2 * EARLY), BF16),
            pltpu.VMEM((4, piece, 2 * late), BF16),
            pltpu.VMEM((4, piece, 2 * local), BF16),
            pltpu.VMEM((6, 2 * piece, 2 * EARLY), BF16),
            pltpu.VMEM((3, 2 * piece, 2 * EARLY), BF16),
            pltpu.VMEM((6, piece, 2 * late), BF16),
            pltpu.VMEM((3, piece, 2 * late), BF16),
            pltpu.VMEM((6, piece, 2 * local), BF16),
            pltpu.VMEM((3, piece, 2 * local), BF16),
            pltpu.VMEM((2, piece, 2 * EARLY), BF16),
            pltpu.SemaphoreType.DMA((8,)),
            pltpu.SemaphoreType.DMA((36,)),
            pltpu.SemaphoreType.DMA((36,)),
        ],
        compiler_params=pltpu.CompilerParams(
            collective_id=0, has_side_effects=True, vmem_limit_bytes=56 * 1024 * 1024
        ),
    )(inputs, middle, out_grad, cached_maps[0], w_value.T, w_out, w_up, w_down)
    in_grad, value_rows, out_rows_t, up_rows, down_rows_t = pl.pallas_call(
        split_kernel,
        out_shape=(
            shape((share, width), BF16),
            shape((piece, local), F32),
            shape((piece, local), F32),
            shape((piece, ff), F32),
            shape((piece, ff), F32),
        ),
        in_specs=[vmem] * 3,
        out_specs=(vmem,) * 5,
    )(*sums)
    return in_grad, value_rows, out_rows_t.T, up_rows, down_rows_t.T


def solution(mesh):
    fused = mesh.shape["img"] == 8 and mesh.shape["head"] == 4
    return jax.shard_map(
        on_device_fused if fused else on_device,
        mesh=mesh,
        in_specs=(
            P("img", None),
            P("img", None),
            P("img", None),
            P("img", "head", None, None),
            P(None, "head"),
            P("head", None),
            P(None, "head"),
            P("head", None),
        ),
        out_specs=(
            P(("img", "head"), None),
            P("img", "head"),
            P("head", "img"),
            P("img", "head"),
            P("head", "img"),
        ),
        check_vma=False,
    )
```

profile of v0, /device:TPU:0, one launch (start us, length us, event | category | flops | bytes accessed | tf_op | source)
XLA Modules:
  0.0 64.5 jit_solution(10577986330345828256)
XLA Ops:
  0.6 61.4 %shard_map.119 = (bf16[64,1280]{1,0:T(8,128)(2,1)}, f32[160,1280]{1,0:T(8,128)}, f32[160,640]{1,0:T(8,128)}) custom-call(bf16[256,1280]{1,0:T(8,128)(2,1)} %inputs_h.1, bf16[256,1280]{1,0:T(8,128)(2,1)} %middle_h.1, bf16[256,1280]{1,0:T(8,128)(2,1)} %out_grad_h.1, bf16[4,256,256]{2,1,0:T(8,128)(2,1)} %bitcast.5, bf16[320,1280]{1,0:T(8,128)(2,1)} %bitcast.4, ...), custom_call_target="tpu_custom_call" | custom-call | tf_op jit(solution)/shard_map/pallas_call | solution.py:420
  62.0 2.5 %shard_map.120 = (bf16[64,1280]{1,0:T(8,128)(2,1)}, f32[160,320]{1,0:T(8,128)}, f32[160,320]{1,0:T(8,128)}, f32[160,640]{1,0:T(8,128)}, f32[160,640]{1,0:T(8,128)}) custom-call(bf16[64,1280]{1,0:T(8,128)(2,1)} %get-tuple-element.13.in_grad, f32[160,1280]{1,0:T(8,128)} %get-tuple-element.14.mlp_sum, f32[160,640]{1,0:T(8,128)} %get-tuple-element.15.att_sum), custom_call_target="tpu_custom_call" | custom-call | tf_op jit(solution)/shard_map/pallas_call | solution.py:472
where the time goes:
time: 64.6 us; the launch traced here: 64.5 us
  Pallas kernels  63.8 us (99%)
    pallas_call x1, Pallas kernels, on_device_fused(): pl.pallas_call(block_kernel, out_shape=(shape((share, width), BF16), shap...  61.4 us
    pallas_call x1, Pallas kernels, on_device_fused(): pl.pallas_call(split_kernel, out_shape=(shape((share, width), BF16), shap...  2.47 us

commit v1 on v0

v1 whole, which is shorter than its diff:
```python
import jax
import jax.numpy as jnp
from jax import lax
from jax.experimental import pallas as pl
from jax.experimental.pallas import tpu as pltpu
from jax.sharding import PartitionSpec as P


def norm_rows(rows):
    centre = rows - jnp.mean(rows, axis=-1, keepdims=True)
    spread = jnp.mean(centre * centre, axis=-1, keepdims=True)
    return centre * lax.rsqrt(spread + 1e-06)


def norm_back(rows, grad):
    centre = rows - jnp.mean(rows, axis=-1, keepdims=True)
    factor = lax.rsqrt(jnp.mean(centre * centre, axis=-1, keepdims=True) + 1e-06)
    normed = centre * factor
    return factor * (
        grad
        - jnp.mean(grad, axis=-1, keepdims=True)
        - normed * jnp.mean(grad * normed, axis=-1, keepdims=True)
    )


def gelu_tanh(pre):
    return jax.nn.gelu(pre, approximate=True)


def on_device(inputs, middle, out_grad, cached_maps, w_value, w_out, w_up, w_down):
    tok_rows = inputs.shape[0]
    heads_here = cached_maps.shape[1]
    share = tok_rows // lax.axis_size("head")
    first = lax.axis_index("head") * share
    maps_here = cached_maps[0]
    normed_in = norm_rows(inputs.astype(jnp.float32)).astype(jnp.bfloat16)
    values = jnp.dot(normed_in, w_value, preferred_element_type=jnp.float32).astype(jnp.bfloat16)
    head_size = values.shape[1] // heads_here
    attended = jnp.einsum(
        "htk,khd->thd",
        maps_here,
        values.reshape(tok_rows, heads_here, head_size),
        preferred_element_type=jnp.float32,
    )
    attended = attended.astype(jnp.bfloat16).reshape(tok_rows, -1)
    middle_f = middle.astype(jnp.float32)
    normed_mid = norm_rows(middle_f).astype(jnp.bfloat16)
    pre = jnp.dot(normed_mid, w_up, preferred_element_type=jnp.float32)
    hidden = gelu_tanh(pre).astype(jnp.bfloat16)
    hidden_grad = jnp.einsum("td,fd->tf", out_grad, w_down, preferred_element_type=jnp.float32)
    pre_grad = jax.vjp(gelu_tanh, pre)[1](hidden_grad)[0].astype(jnp.bfloat16)
    down_term = jnp.einsum("tf,td->fd", hidden, out_grad, preferred_element_type=jnp.float32)
    mid_part = jnp.einsum("tf,df->td", pre_grad, w_up, preferred_element_type=jnp.float32)
    out_rows = lax.dynamic_slice_in_dim(out_grad, first, share, 0).astype(jnp.float32)
    mid_share = lax.psum_scatter(mid_part, "head", scatter_dimension=0, tiled=True)
    mid_own = out_rows + norm_back(lax.dynamic_slice_in_dim(middle_f, first, share, 0), mid_share)
    mid_grad_b = lax.all_gather(mid_own.astype(jnp.bfloat16), "head", axis=0, tiled=True)
    outproj_term = jnp.einsum("te,td->ed", attended, mid_grad_b, preferred_element_type=jnp.float32)
    att_grad = jnp.einsum(
        "td,ed->te", mid_grad_b, w_out, preferred_element_type=jnp.float32
    ).astype(jnp.bfloat16)
    value_grad = jnp.einsum(
        "htk,thd->khd",
        maps_here,
        att_grad.reshape(tok_rows, heads_here, head_size),
        preferred_element_type=jnp.float32,
    )
    value_grad = value_grad.astype(jnp.bfloat16).reshape(tok_rows, -1)
    input_part = jnp.einsum("te,de->td", value_grad, w_value, preferred_element_type=jnp.float32)
    inputs_own = lax.dynamic_slice_in_dim(inputs, first, share, 0).astype(jnp.float32)
    input_share = lax.psum_scatter(input_part, "head", scatter_dimension=0, tiled=True)
    in_grad = (mid_own + norm_back(inputs_own, input_share)).astype(jnp.bfloat16)
    picked = normed_mid
    up_term = jnp.einsum("tr,tf->rf", picked, pre_grad, preferred_element_type=jnp.float32)
    picked = normed_in
    value_term = jnp.einsum("tr,te->re", picked, value_grad, preferred_element_type=jnp.float32)
    grad_down, grad_out = (
        lax.psum_scatter(down_term, "img", scatter_dimension=1, tiled=True),
        lax.psum_scatter(outproj_term, "img", scatter_dimension=1, tiled=True),
    )
    grad_up, grad_value = (
        lax.psum_scatter(up_term, "img", scatter_dimension=0, tiled=True),
        lax.psum_scatter(value_term, "img", scatter_dimension=0, tiled=True),
    )
    return (in_grad, grad_value, grad_out, grad_up, grad_down)


MESH = pl.DeviceIdType.MESH
F32 = jnp.float32
BF16 = jnp.bfloat16
COPIES = 64
GELU_C = 0.7978845608028654


def dot_nn(a, b):
    return lax.dot_general(a, b, (((1,), (0,)), ((), ())), preferred_element_type=F32)


def dot_nt(a, b):
    return lax.dot_general(a, b, (((1,), (1,)), ((), ())), preferred_element_type=F32)


def dot_tn(a, b):
    return lax.dot_general(a, b, (((0,), (0,)), ((), ())), preferred_element_type=F32)


def gelu_and_slope(pre):
    square = pre * pre
    tanh = jnp.tanh(GELU_C * pre * (1.0 + 0.044715 * square))
    half = 0.5 * (1.0 + tanh)
    slope = half + 0.5 * pre * (1.0 - tanh * tanh) * (GELU_C * (1.0 + 3 * 0.044715 * square))
    return pre * half, slope


def block_kernel(
    inputs_h, middle_h, out_grad_h, maps_h, w_value_h, w_out_h, w_up_h, w_down_h,
    in_grad, mlp_sum, att_sum,
    inputs, middle, maps, w_value_t, w_out, w_up, w_down,
    og, nm, ogt, nmt, hid, prg, mlp_part, mlp_send, mlp_recv,
    mp1, ra1, sb1, rb1, mp2, ra2, sb2, rb2, mid_rows, midb,
    nint, nint_p, midbt, midbt_p, attd, attd_p, vgr, vgr_p,
    go_part, go_send, go_recv, go_pass, go_last, gv_part, gv_send, gv_recv, gv_pass, gv_last,
    local_sem, send_sem, recv_sem,
):
    tok, width = inputs.shape
    share = tok // 4
    heads_here = maps.shape[0]
    local = attd.shape[1]
    hdim = local // heads_here
    ff = w_up.shape[1]
    piece = mlp_sum.shape[0]
    img = lax.axis_index("img")
    head = lax.axis_index("head")
    z, x = img // 2, img % 2
    y, c = head // 2, head % 2
    upper, parity = z // 2, z % 2
    x_peer = {"img": z * 2 + (1 - x)}
    side_peer = {"img": (upper * 2 + 1 - parity) * 2 + x}
    cross_peer = {"img": ((1 - upper) * 2 + parity) * 2 + x}
    y_peer = {"head": (1 - y) * 2 + c}
    core_peer = {"head": y * 2 + (1 - c)}
    used = []

    def copy(src, dst, peer):
        sem = len(used)
        used.append(sem)
        return pltpu.make_async_remote_copy(
            src_ref=src, dst_ref=dst, send_sem=send_sem.at[sem], recv_sem=recv_sem.at[sem],
            device_id=peer, device_id_type=MESH,
        )

    started = []

    def send(src, dst, peer):
        one = copy(src, dst, peer)
        one.start()
        started.append(one)
        return one

    def quarter(h):
        return pl.ds(pl.multiple_of(h * share, share), share)

    mine, theirs = quarter(head), quarter((1 - y) * 2 + c)

    barrier = pltpu.get_barrier_semaphore()
    for peer in (x_peer, side_peer, cross_peer, y_peer, core_peer):
        pl.semaphore_signal(barrier, inc=1, device_id=peer, device_id_type=MESH)
    loads = [
        pltpu.make_async_copy(src, dst, local_sem.at[i])
        for i, (src, dst) in enumerate([
            (middle_h, middle), (out_grad_h, og.at[0]), (w_up_h, w_up), (w_down_h, w_down),
            (inputs_h, inputs), (w_value_h, w_value_t), (maps_h, maps), (w_out_h, w_out),
        ])
    ]
    for one in loads:
        one.start()
    loads[0].wait()
    nm[0] = norm_rows(middle[...].astype(F32)).astype(BF16)
    loads[1].wait()
    pl.semaphore_wait(barrier, 5)
    raw = (og, nm)
    slot1 = [send(a.at[0, mine], a.at[1, mine], side_peer) for a in raw]
    slot2 = [send(a.at[0, mine], a.at[2, mine], cross_peer) for a in raw]

    window = pl.ds(pl.multiple_of(upper * (width // 2) + parity * 256, 128), 384)

    def expand(s):
        rows = pl.ds(s * tok, tok)
        value, slope = gelu_and_slope(dot_nn(nm[s], w_up[...]))
        hid[rows] = value.astype(BF16)
        prg[rows] = (slope * dot_nt(og[s], w_down[...])).astype(BF16)

    def turn(s):
        rows = pl.ds(s * tok, tok)
        ogt[:, rows] = og[s, :, window].T
        nmt[:, rows] = nm[s, :, window].T

    def spread_y(s):
        return [send(a.at[s, mine], a.at[s, mine], y_peer) for a in raw]

    def spread_core(s, rows):
        return [send(a.at[s, rows], a.at[s, rows], core_peer) for a in raw]

    def take(copies):
        for one in copies:
            one.wait_recv()

    loads[2].wait()
    loads[3].wait()
    expand(0)
    part = dot_nt(prg[0:tok], w_up[...]).astype(BF16)
    for q in range(4):
        mp1[q % 2, q // 2] = part[q * share:(q + 1) * share]
    core1 = send(mp1.at[1 - c], ra1, core_peer)

    for one in loads[4:]:
        one.wait()
    normed_in = norm_rows(inputs[...].astype(F32)).astype(BF16)
    values = dot_nt(normed_in, w_value_t[...]).astype(BF16)

    core1.wait_recv()
    sb1[...] = (mp1[c].astype(F32) + ra1[...].astype(F32)).astype(BF16)
    y1 = send(sb1, rb1, y_peer)

    column = lax.broadcasted_iota(jnp.int32, (tok, local), 1)

    def own_columns(array, h):
        keep = (column >= h * hdim) & (column < (h + 1) * hdim)
        return jnp.where(keep, array, jnp.zeros_like(array))

    total = dot_nn(maps[0], own_columns(values, 0))
    for h in range(1, heads_here):
        total = total + dot_nn(maps[h], own_columns(values, h))
    attd[...] = total.astype(BF16)
    att_x = send(attd, attd_p, x_peer)

    def halves(array, ref):
        turned = array.T
        for i in range(8):
            ref[i % 2, i // 2] = turned[i * piece:(i + 1) * piece]

    pair = pl.ds(c * 2, 2)
    halves(normed_in, nint)
    nint_x = send(nint.at[1 - x, pair], nint_p.at[pair], x_peer)
    turn(0)

    take(slot1)
    slot1_y = spread_y(1)
    slot1_core = spread_core(1, mine)
    nint_x.wait_recv()
    nint_core = send(nint_p.at[pair], nint_p.at[pair], core_peer)

    y1.wait_recv()
    mid_core = []
    for b in range(2):
        rows = quarter(b * 2 + c)
        grad = mp1[c, b].astype(F32) + ra1[b].astype(F32) + rb1[b].astype(F32)
        own = og[0, rows].astype(F32) + norm_back(middle[rows].astype(F32), grad)
        mid_rows[b] = own
        midb[rows] = own.astype(BF16)
        mid_core.append(send(midb.at[rows], midb.at[rows], core_peer))
    take(slot2)
    slot3 = [send(a.at[2, mine], a.at[3, mine], side_peer) for a in raw]
    slot2_core = spread_core(2, mine)
    take(mid_core)
    halves(midb[...], midbt)
    midbt_x = send(midbt.at[1 - x, pair], midbt_p.at[pair], x_peer)
    att_grad = dot_nt(midb[...], w_out[...]).astype(BF16)
    total = dot_tn(maps[0], own_columns(att_grad, 0))
    for h in range(1, heads_here):
        total = total + dot_tn(maps[h], own_columns(att_grad, h))
    vgr[...] = total.astype(BF16)
    vgr_x = send(vgr, vgr_p, x_peer)
    slot2_y = spread_y(2)
    part = dot_nn(vgr[...], w_value_t[...]).astype(BF16)
    for q in range(4):
        mp2[q % 2, q // 2] = part[q * share:(q + 1) * share]
    core2 = send(mp2.at[1 - c], ra2, core_peer)
    take(slot1_y)
    slot1_core += spread_core(1, theirs)

    midbt_x.wait_recv()
    midbt_core = send(midbt_p.at[pair], midbt_p.at[pair], core_peer)
    take(slot1_core)
    expand(1)
    turn(1)
    core2.wait_recv()
    sb2[...] = (mp2[c, 1 - y].astype(F32) + ra2[1 - y].astype(F32)).astype(BF16)
    y2 = send(sb2, rb2, y_peer)

    def products(left, left_p, right, right_p, part_ref, send_ref):
        flat = 4 * piece
        total = dot_nn(left[x].reshape(flat, tok), right[...])
        total = total + dot_nn(left_p[...].reshape(flat, tok), right_p[...])
        for i in range(4):
            one = total[i * piece:(i + 1) * piece]
            part_ref[i % 2, i // 2] = one
            send_ref[i % 2, i // 2] = one.astype(BF16)

    att_x.wait_recv()
    midbt_core.wait_recv()
    products(midbt, midbt_p, attd, attd_p, go_part, go_send)
    go_side = send(go_send.at[1 - parity], go_recv, side_peer)
    nint_core.wait_recv()
    vgr_x.wait_recv()
    products(nint, nint_p, vgr, vgr_p, gv_part, gv_send)
    gv_side = send(gv_send.at[1 - parity], gv_recv, side_peer)

    take(slot3)
    slot3_y = spread_y(3)
    slot3_core = spread_core(3, mine)
    take(slot2_y)
    slot2_core += spread_core(2, theirs)
    take(slot2_core)
    expand(2)
    turn(2)

    def halve(side, part_ref, recv, pass_ref, last):
        side.wait_recv()
        other = 1 - upper
        pass_ref[...] = (part_ref[parity, other] + recv[other].astype(F32)).astype(BF16)
        return send(pass_ref, last, cross_peer)

    go_cross = halve(go_side, go_part, go_recv, go_pass, go_last)
    gv_cross = halve(gv_side, gv_part, gv_recv, gv_pass, gv_last)

    span = 2 * piece
    rows = pl.ds(pl.multiple_of(parity * 64, 64), span)
    done = slice(0, 3 * tok)
    for i, (left, right) in enumerate(((ogt, hid), (nmt, prg))):
        mlp_part[:, i * ff:(i + 1) * ff] = dot_nn(left[rows, done], right[done])
    y2.wait_recv()
    grad = mp2[c, y].astype(F32) + ra2[y].astype(F32) + rb2[...].astype(F32)
    in_grad[...] = (mid_rows[y] + norm_back(inputs[mine].astype(F32), grad)).astype(BF16)
    take(slot3_y)
    slot3_core += spread_core(3, theirs)
    take(slot3_core)
    expand(3)
    turn(3)
    last = slice(3 * tok, 4 * tok)
    mirror = []
    for i, (left, right) in enumerate(((ogt, hid), (nmt, prg))):
        both = mlp_part[:, i * ff:(i + 1) * ff] + dot_nn(left[rows, last], right[last])
        mlp_part[:, i * ff:(i + 1) * ff] = both
        mlp_send[i, 0] = both[0:piece].astype(BF16)
        mlp_send[i, 1] = both[piece:span].astype(BF16)
        mirror.append(send(mlp_send.at[i, 1 - x], mlp_recv.at[i], x_peer))
    go_cross.wait_recv()
    att_sum[:, 0:local] = go_part[parity, upper] + go_recv[upper].astype(F32) + go_last[...].astype(F32)
    gv_cross.wait_recv()
    att_sum[:, local:2 * local] = gv_part[parity, upper] + gv_recv[upper].astype(F32) + gv_last[...].astype(F32)
    own = pl.ds(pl.multiple_of(x * piece, piece), piece)
    for i in range(2):
        mirror[i].wait_recv()
        mlp_sum[:, i * ff:(i + 1) * ff] = mlp_part[own, i * ff:(i + 1) * ff] + mlp_recv[i].astype(F32)
    for one in started:
        one.wait_send()


def split_kernel(in_grad, mlp_sum, att_sum, in_grad_out, value_rows, out_rows_t, up_rows, down_rows_t):
    local, ff = value_rows.shape[1], up_rows.shape[1]
    in_grad_out[...] = in_grad[...]
    down_rows_t[...] = mlp_sum[:, 0:ff]
    up_rows[...] = mlp_sum[:, ff:2 * ff]
    out_rows_t[...] = att_sum[:, 0:local]
    value_rows[...] = att_sum[:, local:2 * local]


def on_device_fused(inputs, middle, out_grad, cached_maps, w_value, w_out, w_up, w_down):
    tok, width = inputs.shape
    local, ff = w_value.shape[1], w_up.shape[1]
    heads_here = cached_maps.shape[1]
    piece = width // lax.axis_size("img")
    share = tok // 4
    vmem = pl.BlockSpec(memory_space=pltpu.VMEM)
    shape = jax.ShapeDtypeStruct
    sums = pl.pallas_call(
        block_kernel,
        out_shape=(
            shape((share, width), BF16),
            shape((piece, 2 * ff), F32),
            shape((piece, 2 * local), F32),
        ),
        in_specs=[pl.BlockSpec(memory_space=pl.ANY)] * 8,
        out_specs=(vmem,) * 3,
        scratch_shapes=[
            pltpu.VMEM((tok, width), BF16),
            pltpu.VMEM((tok, width), BF16),
            pltpu.VMEM((heads_here, tok, tok), BF16),
            pltpu.VMEM((local, width), BF16),
            pltpu.VMEM((local, width), BF16),
            pltpu.VMEM((width, ff), BF16),
            pltpu.VMEM((ff, width), BF16),
            pltpu.VMEM((4, tok, width), BF16),
            pltpu.VMEM((4, tok, width), BF16),
            pltpu.VMEM((384, 4 * tok), BF16),
            pltpu.VMEM((384, 4 * tok), BF16),
            pltpu.VMEM((4 * tok, ff), BF16),
            pltpu.VMEM((4 * tok, ff), BF16),
            pltpu.VMEM((2 * piece, 2 * ff), F32),
            pltpu.VMEM((2, 2, piece, ff), BF16),
            pltpu.VMEM((2, piece, ff), BF16),
            pltpu.VMEM((2, 2, share, width), BF16),
            pltpu.VMEM((2, share, width), BF16),
            pltpu.VMEM((2, share, width), BF16),
            pltpu.VMEM((2, share, width), BF16),
            pltpu.VMEM((2, 2, share, width), BF16),
            pltpu.VMEM((2, share, width), BF16),
            pltpu.VMEM((share, width), BF16),
            pltpu.VMEM((share, width), BF16),
            pltpu.VMEM((2, share, width), F32),
            pltpu.VMEM((tok, width), BF16),
            pltpu.VMEM((2, 4, piece, tok), BF16),
            pltpu.VMEM((4, piece, tok), BF16),
            pltpu.VMEM((2, 4, piece, tok), BF16),
            pltpu.VMEM((4, piece, tok), BF16),
            pltpu.VMEM((tok, local), BF16),
            pltpu.VMEM((tok, local), BF16),
            pltpu.VMEM((tok, local), BF16),
            pltpu.VMEM((tok, local), BF16),
        ] + [
            pltpu.VMEM((2, 2, piece, local), F32),
            pltpu.VMEM((2, 2, piece, local), BF16),
            pltpu.VMEM((2, piece, local), BF16),
            pltpu.VMEM((piece, local), BF16),
            pltpu.VMEM((piece, local), BF16),
        ] * 2 + [
            pltpu.SemaphoreType.DMA((8,)),
            pltpu.SemaphoreType.DMA((COPIES,)),
            pltpu.SemaphoreType.DMA((COPIES,)),
        ],
        compiler_params=pltpu.CompilerParams(
            collective_id=0, has_side_effects=True, vmem_limit_bytes=56 * 1024 * 1024
        ),
    )(inputs, middle, out_grad, cached_maps[0], w_value.T, w_out, w_up, w_down)
    in_grad, value_rows, out_rows_t, up_rows, down_rows_t = pl.pallas_call(
        split_kernel,
        out_shape=(
            shape((share, width), BF16),
            shape((piece, local), F32),
            shape((piece, local), F32),
            shape((piece, ff), F32),
            shape((piece, ff), F32),
        ),
        in_specs=[vmem] * 3,
        out_specs=(vmem,) * 5,
    )(*sums)
    return in_grad, value_rows, out_rows_t.T, up_rows, down_rows_t.T


def solution(mesh):
    fused = mesh.shape["img"] == 8 and mesh.shape["head"] == 4
    return jax.shard_map(
        on_device_fused if fused else on_device,
        mesh=mesh,
        in_specs=(
            P("img", None),
            P("img", None),
            P("img", None),
            P("img", "head", None, None),
            P(None, "head"),
            P("head", None),
            P(None, "head"),
            P("head", None),
        ),
        out_specs=(
            P(("img", "head"), None),
            P("img", "head"),
            P("head", "img"),
            P("img", "head"),
            P("head", "img"),
        ),
        check_vma=False,
    )
```

time: 64.6 us -> 65.8 us (1.019)
  Pallas kernels: 63.8 us -> 65 us
    pallas_call x1, Pallas kernels: 61.4 us -> 62.5 us  [on_device_fused(): pl.pallas_call(block_kernel, out_shape=(shape((share, width), BF16), shap...]
where the time goes in v1:
time: 65.8 us; the launch traced here: 65.7 us
  Pallas kernels  65 us (99%)
    pallas_call x1, Pallas kernels, on_device_fused(): pl.pallas_call(block_kernel, out_shape=(shape((share, width), BF16), shap...  62.5 us
    pallas_call x1, Pallas kernels, on_device_fused(): pl.pallas_call(split_kernel, out_shape=(shape((share, width), BF16), shap...  2.47 us

profile of v1, /device:TPU:0, one launch (start us, length us, event | category | flops | bytes accessed | tf_op | source)
XLA Modules:
  0.0 65.7 jit_solution(12891990955061891716)
XLA Ops:
  0.6 62.5 %shard_map.119 = (bf16[64,1280]{1,0:T(8,128)(2,1)}, f32[160,1280]{1,0:T(8,128)}, f32[160,640]{1,0:T(8,128)}) custom-call(bf16[256,1280]{1,0:T(8,128)(2,1)} %inputs_h.1, bf16[256,1280]{1,0:T(8,128)(2,1)} %middle_h.1, bf16[256,1280]{1,0:T(8,128)(2,1)} %out_grad_h.1, bf16[4,256,256]{2,1,0:T(8,128)(2,1)} %bitcast.5, bf16[320,1280]{1,0:T(8,128)(2,1)} %bitcast.4, ...), custom_call_target="tpu_custom_call" | custom-call | tf_op jit(solution)/shard_map/pallas_call | solution.py:377
  63.2 2.5 %shard_map.120 = (bf16[64,1280]{1,0:T(8,128)(2,1)}, f32[160,320]{1,0:T(8,128)}, f32[160,320]{1,0:T(8,128)}, f32[160,640]{1,0:T(8,128)}, f32[160,640]{1,0:T(8,128)}) custom-call(bf16[64,1280]{1,0:T(8,128)(2,1)} %get-tuple-element.13.in_grad, f32[160,1280]{1,0:T(8,128)} %get-tuple-element.14.mlp_sum, f32[160,640]{1,0:T(8,128)} %get-tuple-element.15.att_sum), custom_call_target="tpu_custom_call" | custom-call | tf_op jit(solution)/shard_map/pallas_call | solution.py:436

commit v2 on v1

--- a/solution.py
+++ b/solution.py
@@ -114,9 +114,9 @@
 
 def block_kernel(
     inputs_h, middle_h, out_grad_h, maps_h, w_value_h, w_out_h, w_up_h, w_down_h,
-    in_grad, mlp_sum, att_sum,
+    in_grad, gv_sum, go_sum, up_sum, down_sum,
     inputs, middle, maps, w_value_t, w_out, w_up, w_down,
-    og, nm, ogt, nmt, hid, prg, mlp_part, mlp_send, mlp_recv,
+    og, nm, ogt, nmt, hid, prg, grad_h, mlp_part, mlp_send, mlp_recv,
     mp1, ra1, sb1, rb1, mp2, ra2, sb2, rb2, mid_rows, midb,
     nint, nint_p, midbt, midbt_p, attd, attd_p, vgr, vgr_p,
     go_part, go_send, go_recv, go_pass, go_last, gv_part, gv_send, gv_recv, gv_pass, gv_last,
@@ -128,7 +128,7 @@
     local = attd.shape[1]
     hdim = local // heads_here
     ff = w_up.shape[1]
-    piece = mlp_sum.shape[0]
+    piece = up_sum.shape[0]
     img = lax.axis_index("img")
     head = lax.axis_index("head")
     z, x = img // 2, img % 2
@@ -172,15 +172,23 @@
             (inputs_h, inputs), (w_value_h, w_value_t), (maps_h, maps), (w_out_h, w_out),
         ])
     ]
-    for one in loads:
+    for one in loads[:4]:
         one.start()
     loads[0].wait()
+    for one in loads[4:]:
+        one.start()
     nm[0] = norm_rows(middle[...].astype(F32)).astype(BF16)
     loads[1].wait()
     pl.semaphore_wait(barrier, 5)
     raw = (og, nm)
-    slot1 = [send(a.at[0, mine], a.at[1, mine], side_peer) for a in raw]
-    slot2 = [send(a.at[0, mine], a.at[2, mine], cross_peer) for a in raw]
+    direct = ()
+    slot1, slot2 = [], []
+
+    def first_send(a):
+        slot2.append(send(a.at[0, mine], a.at[2, mine], cross_peer))
+        slot1.append([send(a.at[0, mine], a.at[1, mine], side_peer)])
+
+    first_send(og)
 
     window = pl.ds(pl.multiple_of(upper * (width // 2) + parity * 256, 128), 384)
 
@@ -195,11 +203,26 @@
         ogt[:, rows] = og[s, :, window].T
         nmt[:, rows] = nm[s, :, window].T
 
-    def spread_y(s):
-        return [send(a.at[s, mine], a.at[s, mine], y_peer) for a in raw]
-
-    def spread_core(s, rows):
-        return [send(a.at[s, rows], a.at[s, rows], core_peer) for a in raw]
+    core_in = {(s, i): [] for s in (1, 2, 3) for i in range(2)}
+    y_in, slot3 = {}, {}
+
+    def across_core(s, i, rows):
+        core_in[s, i].append(send(raw[i].at[s, rows], raw[i].at[s, rows], core_peer))
+
+    def landed(s, i):
+        (slot1[i][0] if s == 1 else slot2[i] if s == 2 else slot3[i]).wait_recv()
+        if s == 2:
+            slot3[i] = send(raw[i].at[2, mine], raw[i].at[3, mine], side_peer)
+        if s != 1 or i not in direct:
+            y_in[s, i] = send(raw[i].at[s, mine], raw[i].at[s, mine], y_peer)
+        across_core(s, i, mine)
+
+    def other_landed(s, i):
+        (slot1[i][1] if s == 1 and i in direct else y_in[s, i]).wait_recv()
+        across_core(s, i, theirs)
+
+    def ready(s):
+        take(core_in[s, 0] + core_in[s, 1])
 
     def take(copies):
         for one in copies:
@@ -212,6 +235,7 @@
     for q in range(4):
         mp1[q % 2, q // 2] = part[q * share:(q + 1) * share]
     core1 = send(mp1.at[1 - c], ra1, core_peer)
+    first_send(nm)
 
     for one in loads[4:]:
         one.wait()
@@ -243,15 +267,10 @@
     halves(normed_in, nint)
     nint_x = send(nint.at[1 - x, pair], nint_p.at[pair], x_peer)
     turn(0)
-
-    take(slot1)
-    slot1_y = spread_y(1)
-    slot1_core = spread_core(1, mine)
-    nint_x.wait_recv()
-    nint_core = send(nint_p.at[pair], nint_p.at[pair], core_peer)
-
+    landed(2, 0)
+    landed(1, 0)
+    mid_core = []
     y1.wait_recv()
-    mid_core = []
     for b in range(2):
         rows = quarter(b * 2 + c)
         grad = mp1[c, b].astype(F32) + ra1[b].astype(F32) + rb1[b].astype(F32)
@@ -259,9 +278,8 @@
         mid_rows[b] = own
         midb[rows] = own.astype(BF16)
         mid_core.append(send(midb.at[rows], midb.at[rows], core_peer))
-    take(slot2)
-    slot3 = [send(a.at[2, mine], a.at[3, mine], side_peer) for a in raw]
-    slot2_core = spread_core(2, mine)
+    nint_x.wait_recv()
+    nint_core = send(nint_p.at[pair], nint_p.at[pair], core_peer)
     take(mid_core)
     halves(midb[...], midbt)
     midbt_x = send(midbt.at[1 - x, pair], midbt_p.at[pair], x_peer)
@@ -271,22 +289,14 @@
         total = total + dot_tn(maps[h], own_columns(att_grad, h))
     vgr[...] = total.astype(BF16)
     vgr_x = send(vgr, vgr_p, x_peer)
-    slot2_y = spread_y(2)
+    landed(2, 1)
+    landed(1, 1)
+    other_landed(2, 0)
+    other_landed(1, 0)
     part = dot_nn(vgr[...], w_value_t[...]).astype(BF16)
     for q in range(4):
         mp2[q % 2, q // 2] = part[q * share:(q + 1) * share]
     core2 = send(mp2.at[1 - c], ra2, core_peer)
-    take(slot1_y)
-    slot1_core += spread_core(1, theirs)
-
-    midbt_x.wait_recv()
-    midbt_core = send(midbt_p.at[pair], midbt_p.at[pair], core_peer)
-    take(slot1_core)
-    expand(1)
-    turn(1)
-    core2.wait_recv()
-    sb2[...] = (mp2[c, 1 - y].astype(F32) + ra2[1 - y].astype(F32)).astype(BF16)
-    y2 = send(sb2, rb2, y_peer)
 
     def products(left, left_p, right, right_p, part_ref, send_ref):
         flat = 4 * piece
@@ -297,6 +307,8 @@
             part_ref[i % 2, i // 2] = one
             send_ref[i % 2, i // 2] = one.astype(BF16)
 
+    midbt_x.wait_recv()
+    midbt_core = send(midbt_p.at[pair], midbt_p.at[pair], core_peer)
     att_x.wait_recv()
     midbt_core.wait_recv()
     products(midbt, midbt_p, attd, attd_p, go_part, go_send)
@@ -305,13 +317,17 @@
     vgr_x.wait_recv()
     products(nint, nint_p, vgr, vgr_p, gv_part, gv_send)
     gv_side = send(gv_send.at[1 - parity], gv_recv, side_peer)
-
-    take(slot3)
-    slot3_y = spread_y(3)
-    slot3_core = spread_core(3, mine)
-    take(slot2_y)
-    slot2_core += spread_core(2, theirs)
-    take(slot2_core)
+    landed(3, 0)
+    other_landed(2, 1)
+    other_landed(1, 1)
+    landed(3, 1)
+    core2.wait_recv()
+    sb2[...] = (mp2[c, 1 - y].astype(F32) + ra2[1 - y].astype(F32)).astype(BF16)
+    y2 = send(sb2, rb2, y_peer)
+    ready(1)
+    expand(1)
+    turn(1)
+    ready(2)
     expand(2)
     turn(2)
 
@@ -321,49 +337,57 @@
         pass_ref[...] = (part_ref[parity, other] + recv[other].astype(F32)).astype(BF16)
         return send(pass_ref, last, cross_peer)
 
+    other_landed(3, 0)
     go_cross = halve(go_side, go_part, go_recv, go_pass, go_last)
-    gv_cross = halve(gv_side, gv_part, gv_recv, gv_pass, gv_last)
-
     span = 2 * piece
     rows = pl.ds(pl.multiple_of(parity * 64, 64), span)
     done = slice(0, 3 * tok)
     for i, (left, right) in enumerate(((ogt, hid), (nmt, prg))):
         mlp_part[:, i * ff:(i + 1) * ff] = dot_nn(left[rows, done], right[done])
-    y2.wait_recv()
-    grad = mp2[c, y].astype(F32) + ra2[y].astype(F32) + rb2[...].astype(F32)
-    in_grad[...] = (mid_rows[y] + norm_back(inputs[mine].astype(F32), grad)).astype(BF16)
-    take(slot3_y)
-    slot3_core += spread_core(3, theirs)
-    take(slot3_core)
-    expand(3)
-    turn(3)
+    take(core_in[3, 0])
+    grad_h[...] = dot_nt(og[3], w_down[...])
+    ogt[:, 3 * tok:4 * tok] = og[3, :, window].T
+    other_landed(3, 1)
+    take(core_in[3, 1])
     last = slice(3 * tok, 4 * tok)
     mirror = []
-    for i, (left, right) in enumerate(((ogt, hid), (nmt, prg))):
+
+    def finish(i, left, right):
         both = mlp_part[:, i * ff:(i + 1) * ff] + dot_nn(left[rows, last], right[last])
         mlp_part[:, i * ff:(i + 1) * ff] = both
         mlp_send[i, 0] = both[0:piece].astype(BF16)
         mlp_send[i, 1] = both[piece:span].astype(BF16)
         mirror.append(send(mlp_send.at[i, 1 - x], mlp_recv.at[i], x_peer))
+
+    value, slope = gelu_and_slope(dot_nn(nm[3], w_up[...]))
+    hid[last] = value.astype(BF16)
+    finish(0, ogt, hid)
+    gv_cross = halve(gv_side, gv_part, gv_recv, gv_pass, gv_last)
+    prg[last] = (slope * grad_h[...]).astype(BF16)
+    nmt[:, last] = nm[3, :, window].T
+    finish(1, nmt, prg)
+    y2.wait_recv()
+    grad = mp2[c, y].astype(F32) + ra2[y].astype(F32) + rb2[...].astype(F32)
+    in_grad[...] = (mid_rows[y] + norm_back(inputs[mine].astype(F32), grad)).astype(BF16)
     go_cross.wait_recv()
-    att_sum[:, 0:local] = go_part[parity, upper] + go_recv[upper].astype(F32) + go_last[...].astype(F32)
+    go_sum[...] = go_part[parity, upper] + go_recv[upper].astype(F32) + go_last[...].astype(F32)
     gv_cross.wait_recv()
-    att_sum[:, local:2 * local] = gv_part[parity, upper] + gv_recv[upper].astype(F32) + gv_last[...].astype(F32)
+    gv_sum[...] = gv_part[parity, upper] + gv_recv[upper].astype(F32) + gv_last[...].astype(F32)
     own = pl.ds(pl.multiple_of(x * piece, piece), piece)
-    for i in range(2):
+    for i, total in enumerate((down_sum, up_sum)):
         mirror[i].wait_recv()
-        mlp_sum[:, i * ff:(i + 1) * ff] = mlp_part[own, i * ff:(i + 1) * ff] + mlp_recv[i].astype(F32)
+        total[...] = mlp_part[own, i * ff:(i + 1) * ff] + mlp_recv[i].astype(F32)
     for one in started:
         one.wait_send()
 
 
-def split_kernel(in_grad, mlp_sum, att_sum, in_grad_out, value_rows, out_rows_t, up_rows, down_rows_t):
-    local, ff = value_rows.shape[1], up_rows.shape[1]
-    in_grad_out[...] = in_grad[...]
-    down_rows_t[...] = mlp_sum[:, 0:ff]
-    up_rows[...] = mlp_sum[:, ff:2 * ff]
-    out_rows_t[...] = att_sum[:, 0:local]
-    value_rows[...] = att_sum[:, local:2 * local]
+def copy_kernel(*refs):
+    sem = refs[-1]
+    moves = [pltpu.make_async_copy(refs[i], refs[5 + i], sem.at[i]) for i in range(5)]
+    for one in moves:
+        one.start()
+    for one in moves:
+        one.wait()
 
 
 def on_device_fused(inputs, middle, out_grad, cached_maps, w_value, w_out, w_up, w_down):
@@ -374,15 +398,18 @@
     share = tok // 4
     vmem = pl.BlockSpec(memory_space=pltpu.VMEM)
     shape = jax.ShapeDtypeStruct
+    results = (
+        shape((share, width), BF16),
+        shape((piece, local), F32),
+        shape((piece, local), F32),
+        shape((piece, ff), F32),
+        shape((piece, ff), F32),
+    )
     sums = pl.pallas_call(
         block_kernel,
-        out_shape=(
-            shape((share, width), BF16),
-            shape((piece, 2 * ff), F32),
-            shape((piece, 2 * local), F32),
-        ),
+        out_shape=results,
         in_specs=[pl.BlockSpec(memory_space=pl.ANY)] * 8,
-        out_specs=(vmem,) * 3,
+        out_specs=(vmem,) * 5,
         scratch_shapes=[
             pltpu.VMEM((tok, width), BF16),
             pltpu.VMEM((tok, width), BF16),
@@ -397,6 +424,7 @@
             pltpu.VMEM((384, 4 * tok), BF16),
             pltpu.VMEM((4 * tok, ff), BF16),
             pltpu.VMEM((4 * tok, ff), BF16),
+            pltpu.VMEM((tok, ff), F32),
             pltpu.VMEM((2 * piece, 2 * ff), F32),
             pltpu.VMEM((2, 2, piece, ff), BF16),
             pltpu.VMEM((2, piece, ff), BF16),
@@ -433,17 +461,13 @@
             collective_id=0, has_side_effects=True, vmem_limit_bytes=56 * 1024 * 1024
         ),
     )(inputs, middle, out_grad, cached_maps[0], w_value.T, w_out, w_up, w_down)
+    anywhere = pl.BlockSpec(memory_space=pl.ANY)
     in_grad, value_rows, out_rows_t, up_rows, down_rows_t = pl.pallas_call(
-        split_kernel,
-        out_shape=(
-            shape((share, width), BF16),
-            shape((piece, local), F32),
-            shape((piece, local), F32),
-            shape((piece, ff), F32),
-            shape((piece, ff), F32),
-        ),
-        in_specs=[vmem] * 3,
-        out_specs=(vmem,) * 5,
+        copy_kernel,
+        out_shape=results,
+        in_specs=[vmem] * 5,
+        out_specs=(anywhere,) * 5,
+        scratch_shapes=[pltpu.SemaphoreType.DMA((5,))],
     )(*sums)
     return in_grad, value_rows, out_rows_t.T, up_rows, down_rows_t.T
 

time: 65.8 us -> 57 us (0.87)
  Pallas kernels: 65 us -> 56.1 us
    pallas_call x2, Pallas kernels: 65 us -> 56.1 us  [the longest x1 53.6 us: on_device_fused(): pl.pallas_call(block_kernel, out_shape=results, in_specs=[pl.BlockSpec(me...]
where the time goes in v2:
time: 57 us; the launch traced here: 56.8 us
  Pallas kernels  56.1 us (98%)
  between operations  0.64 us (1%)
    pallas_call x1, Pallas kernels, on_device_fused(): pl.pallas_call(block_kernel, out_shape=results, in_specs=[pl.BlockSpec(me...  53.6 us
    pallas_call x1, Pallas kernels, on_device_fused(): pl.pallas_call(copy_kernel, out_shape=results, in_specs=[vmem] * 5, out_s...  2.53 us

profile of v2, /device:TPU:0, one launch (start us, length us, event | category | flops | bytes accessed | tf_op | source)
XLA Modules:
  0.0 56.8 jit_solution(2890569128933670828)
XLA Ops:
  0.6 53.6 %shard_map.119 = (bf16[64,1280]{1,0:T(8,128)(2,1)}, f32[160,320]{1,0:T(8,128)}, f32[160,320]{1,0:T(8,128)}, f32[160,640]{1,0:T(8,128)}, f32[160,640]{1,0:T(8,128)}) custom-call(bf16[256,1280]{1,0:T(8,128)(2,1)} %inputs_h.1, bf16[256,1280]{1,0:T(8,128)(2,1)} %middle_h.1, bf16[256,1280]{1,0:T(8,128)(2,1)} %out_grad_h.1, bf16[4,256,256]{2,1,0:T(8,128)(2,1)} %bitcast.5, ...), custom_call_target="tpu_custom_call" | custom-call | tf_op jit(solution)/shard_map/pallas_call | solution.py:408
  54.3 2.5 %shard_map.120 = (bf16[64,1280]{1,0:T(8,128)(2,1)}, f32[160,320]{1,0:T(8,128)}, f32[160,320]{1,0:T(8,128)}, f32[160,640]{1,0:T(8,128)}, f32[160,640]{1,0:T(8,128)}) custom-call(bf16[64,1280]{1,0:T(8,128)(2,1)} %get-tuple-element.15.refs_0_, f32[160,320]{1,0:T(8,128)} %get-tuple-element.16.refs_1_, f32[160,320]{1,0:T(8,128)} %get-tuple-element.17.refs_2_, ...), custom_call_target="tpu_custom_call" | custom-call | tf_op jit(solution)/shard_map/pallas_call | solution.py:465

commit v3 on v2

--- a/solution.py
+++ b/solution.py
@@ -114,9 +114,9 @@
 
 def block_kernel(
     inputs_h, middle_h, out_grad_h, maps_h, w_value_h, w_out_h, w_up_h, w_down_h,
-    in_grad, gv_sum, go_sum, up_sum, down_sum,
+    in_grad_h, gv_sum_h, go_sum_h, mlp_own_h, mlp_recv,
     inputs, middle, maps, w_value_t, w_out, w_up, w_down,
-    og, nm, ogt, nmt, hid, prg, grad_h, mlp_part, mlp_send, mlp_recv,
+    og, nm, og_cut, ogt, nmt, hid, prg, grad_h, in_grad, gv_sum, go_sum, mlp_part, mlp_send,
     mp1, ra1, sb1, rb1, mp2, ra2, sb2, rb2, mid_rows, midb,
     nint, nint_p, midbt, midbt_p, attd, attd_p, vgr, vgr_p,
     go_part, go_send, go_recv, go_pass, go_last, gv_part, gv_send, gv_recv, gv_pass, gv_last,
@@ -128,7 +128,7 @@
     local = attd.shape[1]
     hdim = local // heads_here
     ff = w_up.shape[1]
-    piece = up_sum.shape[0]
+    piece = mlp_send.shape[2]
     img = lax.axis_index("img")
     head = lax.axis_index("head")
     z, x = img // 2, img % 2
@@ -180,7 +180,7 @@
     nm[0] = norm_rows(middle[...].astype(F32)).astype(BF16)
     loads[1].wait()
     pl.semaphore_wait(barrier, 5)
-    raw = (og, nm)
+    raw = (nm, og)
     direct = ()
     slot1, slot2 = [], []
 
@@ -188,7 +188,7 @@
         slot2.append(send(a.at[0, mine], a.at[2, mine], cross_peer))
         slot1.append([send(a.at[0, mine], a.at[1, mine], side_peer)])
 
-    first_send(og)
+    first_send(nm)
 
     window = pl.ds(pl.multiple_of(upper * (width // 2) + parity * 256, 128), 384)
 
@@ -204,13 +204,16 @@
         nmt[:, rows] = nm[s, :, window].T
 
     core_in = {(s, i): [] for s in (1, 2, 3) for i in range(2)}
-    y_in, slot3 = {}, {}
+    y_in, slot3, cut = {}, {}, {}
+    side_window = pl.ds(pl.multiple_of(upper * (width // 2) + (1 - parity) * 256, 128), 384)
 
     def across_core(s, i, rows):
         core_in[s, i].append(send(raw[i].at[s, rows], raw[i].at[s, rows], core_peer))
 
     def landed(s, i):
         (slot1[i][0] if s == 1 else slot2[i] if s == 2 else slot3[i]).wait_recv()
+        if s == 2 and i == 1:
+            cut["first"] = send(og.at[2, mine, side_window], og_cut.at[mine], side_peer)
         if s == 2:
             slot3[i] = send(raw[i].at[2, mine], raw[i].at[3, mine], side_peer)
         if s != 1 or i not in direct:
@@ -220,6 +223,15 @@
     def other_landed(s, i):
         (slot1[i][1] if s == 1 and i in direct else y_in[s, i]).wait_recv()
         across_core(s, i, theirs)
+
+    def cut_landed():
+        cut["first"].wait_recv()
+        cut["y"] = send(og_cut.at[mine], og_cut.at[mine], y_peer)
+        cut["core"] = [send(og_cut.at[mine], og_cut.at[mine], core_peer)]
+
+    def other_cut_landed():
+        cut["y"].wait_recv()
+        cut["core"].append(send(og_cut.at[theirs], og_cut.at[theirs], core_peer))
 
     def ready(s):
         take(core_in[s, 0] + core_in[s, 1])
@@ -235,7 +247,7 @@
     for q in range(4):
         mp1[q % 2, q // 2] = part[q * share:(q + 1) * share]
     core1 = send(mp1.at[1 - c], ra1, core_peer)
-    first_send(nm)
+    first_send(og)
 
     for one in loads[4:]:
         one.wait()
@@ -320,6 +332,7 @@
     landed(3, 0)
     other_landed(2, 1)
     other_landed(1, 1)
+    cut_landed()
     landed(3, 1)
     core2.wait_recv()
     sb2[...] = (mp2[c, 1 - y].astype(F32) + ra2[1 - y].astype(F32)).astype(BF16)
@@ -344,11 +357,7 @@
     done = slice(0, 3 * tok)
     for i, (left, right) in enumerate(((ogt, hid), (nmt, prg))):
         mlp_part[:, i * ff:(i + 1) * ff] = dot_nn(left[rows, done], right[done])
-    take(core_in[3, 0])
-    grad_h[...] = dot_nt(og[3], w_down[...])
-    ogt[:, 3 * tok:4 * tok] = og[3, :, window].T
-    other_landed(3, 1)
-    take(core_in[3, 1])
+    other_cut_landed()
     last = slice(3 * tok, 4 * tok)
     mirror = []
 
@@ -359,34 +368,64 @@
         mlp_send[i, 1] = both[piece:span].astype(BF16)
         mirror.append(send(mlp_send.at[i, 1 - x], mlp_recv.at[i], x_peer))
 
+    take(core_in[3, 0])
     value, slope = gelu_and_slope(dot_nn(nm[3], w_up[...]))
     hid[last] = value.astype(BF16)
+    grad_h[...] = slope
+    take(cut["core"])
+    ogt[:, last] = og_cut[...].T
     finish(0, ogt, hid)
+    nmt[:, last] = nm[3, :, window].T
+    other_landed(3, 1)
     gv_cross = halve(gv_side, gv_part, gv_recv, gv_pass, gv_last)
-    prg[last] = (slope * grad_h[...]).astype(BF16)
-    nmt[:, last] = nm[3, :, window].T
+    take(core_in[3, 1])
+    prg[last] = (grad_h[...] * dot_nt(og[3], w_down[...])).astype(BF16)
     finish(1, nmt, prg)
     y2.wait_recv()
     grad = mp2[c, y].astype(F32) + ra2[y].astype(F32) + rb2[...].astype(F32)
     in_grad[...] = (mid_rows[y] + norm_back(inputs[mine].astype(F32), grad)).astype(BF16)
+    stores = []
+
+    def store(src, dst):
+        one = pltpu.make_async_copy(src, dst, local_sem.at[8 + len(stores)])
+        one.start()
+        stores.append(one)
+
+    own = pl.ds(pl.multiple_of(x * piece, piece), piece)
+    store(in_grad, in_grad_h)
+    for i in range(2):
+        store(mlp_part.at[own, pl.ds(i * ff, ff)], mlp_own_h.at[i])
     go_cross.wait_recv()
     go_sum[...] = go_part[parity, upper] + go_recv[upper].astype(F32) + go_last[...].astype(F32)
+    store(go_sum, go_sum_h)
     gv_cross.wait_recv()
     gv_sum[...] = gv_part[parity, upper] + gv_recv[upper].astype(F32) + gv_last[...].astype(F32)
-    own = pl.ds(pl.multiple_of(x * piece, piece), piece)
-    for i, total in enumerate((down_sum, up_sum)):
-        mirror[i].wait_recv()
-        total[...] = mlp_part[own, i * ff:(i + 1) * ff] + mlp_recv[i].astype(F32)
+    store(gv_sum, gv_sum_h)
+    for one in stores:
+        one.wait()
+    for one in mirror:
+        one.wait_recv()
     for one in started:
         one.wait_send()
 
 
-def copy_kernel(*refs):
-    sem = refs[-1]
-    moves = [pltpu.make_async_copy(refs[i], refs[5 + i], sem.at[i]) for i in range(5)]
-    for one in moves:
+def last_sums_kernel(
+    in_grad, gv_sum, go_sum, mlp_own, mlp_recv, in_grad_h, gv_sum_h, go_sum_h, up_sum_h, down_sum_h, sums, sem
+):
+    stores = []
+
+    def store(src, dst):
+        one = pltpu.make_async_copy(src, dst, sem.at[len(stores)])
         one.start()
-    for one in moves:
+        stores.append(one)
+
+    for i, dst in enumerate((down_sum_h, up_sum_h)):
+        sums[i] = mlp_own[i] + mlp_recv[i].astype(F32)
+        store(sums.at[i], dst)
+    store(in_grad, in_grad_h)
+    store(gv_sum, gv_sum_h)
+    store(go_sum, go_sum_h)
+    for one in stores:
         one.wait()
 
 
@@ -397,6 +436,7 @@
     piece = width // lax.axis_size("img")
     share = tok // 4
     vmem = pl.BlockSpec(memory_space=pltpu.VMEM)
+    anywhere = pl.BlockSpec(memory_space=pl.ANY)
     shape = jax.ShapeDtypeStruct
     results = (
         shape((share, width), BF16),
@@ -407,9 +447,9 @@
     )
     sums = pl.pallas_call(
         block_kernel,
-        out_shape=results,
-        in_specs=[pl.BlockSpec(memory_space=pl.ANY)] * 8,
-        out_specs=(vmem,) * 5,
+        out_shape=results[:3] + (shape((2, piece, ff), F32), shape((2, piece, ff), BF16)),
+        in_specs=[anywhere] * 8,
+        out_specs=(anywhere,) * 5,
         scratch_shapes=[
             pltpu.VMEM((tok, width), BF16),
             pltpu.VMEM((tok, width), BF16),
@@ -420,14 +460,17 @@
             pltpu.VMEM((ff, width), BF16),
             pltpu.VMEM((4, tok, width), BF16),
             pltpu.VMEM((4, tok, width), BF16),
+            pltpu.VMEM((tok, 384), BF16),
             pltpu.VMEM((384, 4 * tok), BF16),
             pltpu.VMEM((384, 4 * tok), BF16),
             pltpu.VMEM((4 * tok, ff), BF16),
             pltpu.VMEM((4 * tok, ff), BF16),
             pltpu.VMEM((tok, ff), F32),
+            pltpu.VMEM((share, width), BF16),
+            pltpu.VMEM((piece, local), F32),
+            pltpu.VMEM((piece, local), F32),
             pltpu.VMEM((2 * piece, 2 * ff), F32),
             pltpu.VMEM((2, 2, piece, ff), BF16),
-            pltpu.VMEM((2, piece, ff), BF16),
             pltpu.VMEM((2, 2, share, width), BF16),
             pltpu.VMEM((2, share, width), BF16),
             pltpu.VMEM((2, share, width), BF16),
@@ -453,7 +496,7 @@
             pltpu.VMEM((piece, local), BF16),
             pltpu.VMEM((piece, local), BF16),
         ] * 2 + [
-            pltpu.SemaphoreType.DMA((8,)),
+            pltpu.SemaphoreType.DMA((13,)),
             pltpu.SemaphoreType.DMA((COPIES,)),
             pltpu.SemaphoreType.DMA((COPIES,)),
         ],
@@ -461,13 +504,12 @@
             collective_id=0, has_side_effects=True, vmem_limit_bytes=56 * 1024 * 1024
         ),
     )(inputs, middle, out_grad, cached_maps[0], w_value.T, w_out, w_up, w_down)
-    anywhere = pl.BlockSpec(memory_space=pl.ANY)
     in_grad, value_rows, out_rows_t, up_rows, down_rows_t = pl.pallas_call(
-        copy_kernel,
+        last_sums_kernel,
         out_shape=results,
         in_specs=[vmem] * 5,
         out_specs=(anywhere,) * 5,
-        scratch_shapes=[pltpu.SemaphoreType.DMA((5,))],
+        scratch_shapes=[pltpu.VMEM((2, piece, ff), F32), pltpu.SemaphoreType.DMA((5,))],
     )(*sums)
     return in_grad, value_rows, out_rows_t.T, up_rows, down_rows_t.T
 

time: 57 us -> 55 us (0.965)
  Pallas kernels: 56.1 us -> 54.2 us
    pallas_call x2, Pallas kernels: 56.1 us -> 54.2 us  [the longest x1 51.5 us: on_device_fused(): pl.pallas_call(block_kernel, out_shape=results[:3] + (shape((2, piece, ff...]
where the time goes in v3:
time: 55 us; the launch traced here: 54.8 us
  Pallas kernels  54.2 us (99%)
  between operations  0.64 us (1%)
    pallas_call x1, Pallas kernels, on_device_fused(): pl.pallas_call(block_kernel, out_shape=results[:3] + (shape((2, piece, ff...  51.5 us
    pallas_call x1, Pallas kernels, on_device_fused(): pl.pallas_call(last_sums_kernel, out_shape=results, in_specs=[vmem] * 5,...  2.68 us

profile of v3, /device:TPU:0, one launch (start us, length us, event | category | flops | bytes accessed | tf_op | source)
XLA Modules:
  0.0 54.8 jit_solution(8900104801588823225)
XLA Ops:
  0.6 51.5 %shard_map.119 = (bf16[64,1280]{1,0:T(8,128)(2,1)}, f32[160,320]{1,0:T(8,128)}, f32[160,320]{1,0:T(8,128)}, f32[2,160,640]{2,1,0:T(8,128)}, bf16[2,160,640]{2,1,0:T(8,128)(2,1)}) custom-call(bf16[256,1280]{1,0:T(8,128)(2,1)} %inputs_h.1, bf16[256,1280]{1,0:T(8,128)(2,1)} %middle_h.1, bf16[256,1280]{1,0:T(8,128)(2,1)} %out_grad_h.1, ...), custom_call_target="tpu_custom_call" | custom-call | tf_op jit(solution)/shard_map/pallas_call | solution.py:448
  52.1 2.7 %shard_map.120 = (bf16[64,1280]{1,0:T(8,128)(2,1)}, f32[160,320]{1,0:T(8,128)}, f32[160,320]{1,0:T(8,128)}, f32[160,640]{1,0:T(8,128)}, f32[160,640]{1,0:T(8,128)}) custom-call(bf16[64,1280]{1,0:T(8,128)(2,1)} %get-tuple-element.15.in_grad, f32[160,320]{1,0:T(8,128)} %get-tuple-element.16.gv_sum, f32[160,320]{1,0:T(8,128)} %get-tuple-element.17.go_sum, ...), custom_call_target="tpu_custom_call" | custom-call | tf_op jit(solution)/shard_map/pallas_call | solution.py:507

commit v4 on v3

--- a/solution.py
+++ b/solution.py
@@ -189,6 +189,7 @@
         slot1.append([send(a.at[0, mine], a.at[1, mine], side_peer)])
 
     first_send(nm)
+    first_send(og)
 
     window = pl.ds(pl.multiple_of(upper * (width // 2) + parity * 256, 128), 384)
 
@@ -247,7 +248,6 @@
     for q in range(4):
         mp1[q % 2, q // 2] = part[q * share:(q + 1) * share]
     core1 = send(mp1.at[1 - c], ra1, core_peer)
-    first_send(og)
 
     for one in loads[4:]:
         one.wait()
@@ -334,9 +334,6 @@
     other_landed(1, 1)
     cut_landed()
     landed(3, 1)
-    core2.wait_recv()
-    sb2[...] = (mp2[c, 1 - y].astype(F32) + ra2[1 - y].astype(F32)).astype(BF16)
-    y2 = send(sb2, rb2, y_peer)
     ready(1)
     expand(1)
     turn(1)
@@ -377,6 +374,9 @@
     finish(0, ogt, hid)
     nmt[:, last] = nm[3, :, window].T
     other_landed(3, 1)
+    core2.wait_recv()
+    sb2[...] = (mp2[c, 1 - y].astype(F32) + ra2[1 - y].astype(F32)).astype(BF16)
+    y2 = send(sb2, rb2, y_peer)
     gv_cross = halve(gv_side, gv_part, gv_recv, gv_pass, gv_last)
     take(core_in[3, 1])
     prg[last] = (grad_h[...] * dot_nt(og[3], w_down[...])).astype(BF16)

time: 55 us -> 55 us (level)
  no operation moved by 1% of the time
where the time goes in v4:
time: 55 us; the launch traced here: 54.8 us
  Pallas kernels  54.2 us (99%)
  between operations  0.64 us (1%)
    pallas_call x1, Pallas kernels, on_device_fused(): pl.pallas_call(block_kernel, out_shape=results[:3] + (shape((2, piece, ff...  51.5 us
    pallas_call x1, Pallas kernels, on_device_fused(): pl.pallas_call(last_sums_kernel, out_shape=results, in_specs=[vmem] * 5,...  2.68 us

profile of v4, /device:TPU:0, one launch (start us, length us, event | category | flops | bytes accessed | tf_op | source)
XLA Modules:
  0.0 54.8 jit_solution(1600179580976702269)
XLA Ops:
  0.6 51.5 %shard_map.119 = (bf16[64,1280]{1,0:T(8,128)(2,1)}, f32[160,320]{1,0:T(8,128)}, f32[160,320]{1,0:T(8,128)}, f32[2,160,640]{2,1,0:T(8,128)}, bf16[2,160,640]{2,1,0:T(8,128)(2,1)}) custom-call(bf16[256,1280]{1,0:T(8,128)(2,1)} %inputs_h.1, bf16[256,1280]{1,0:T(8,128)(2,1)} %middle_h.1, bf16[256,1280]{1,0:T(8,128)(2,1)} %out_grad_h.1, ...), custom_call_target="tpu_custom_call" | custom-call | tf_op jit(solution)/shard_map/pallas_call | solution.py:448
  52.1 2.7 %shard_map.120 = (bf16[64,1280]{1,0:T(8,128)(2,1)}, f32[160,320]{1,0:T(8,128)}, f32[160,320]{1,0:T(8,128)}, f32[160,640]{1,0:T(8,128)}, f32[160,640]{1,0:T(8,128)}) custom-call(bf16[64,1280]{1,0:T(8,128)(2,1)} %get-tuple-element.15.in_grad, f32[160,320]{1,0:T(8,128)} %get-tuple-element.16.gv_sum, f32[160,320]{1,0:T(8,128)} %get-tuple-element.17.go_sum, ...), custom_call_target="tpu_custom_call" | custom-call | tf_op jit(solution)/shard_map/pallas_call | solution.py:507
